TPU v7x, 256 devices: a whole 4x4x8 slice. The times are simulated.
256 devices in a mesh: rows: 16 (over z, core), feat: 16 (over x, y).
Axes of the slice: x: 4, y: 4, z: 8, core: 2. Of those that a mesh axis runs over, the one named last changes fastest.
Arguments:
- features: bfloat16 [16384, 16384], P('rows', 'feat'), may hold values from -0.046875 to 0.046875
- inverse_gram: float32 [16384, 1024], P('feat'), as said below
- targets: float32 [128, 16384], P('feat', 'rows'), may hold values from -6 to 6
Outputs:
- weights: float32 [128, 16384], P(None, 'feat')
- residual: float32 [128, 16384], P('feat', 'rows')
Inputs may be any that keep to these rules, and one draw needn't show every extreme that they name: Each block of inverse_gram is symmetric.
All inputs are finite; a program needn't handle non-finite values.
Results may differ from a plain program's by a relative error of at most 0.007.
Values sent between devices are 32-bit elements; how exact they have to be, the bound alone decides.
No kernel may reach another device: no remote copies, remote signals or barrier semaphores. Data moves between devices by JAX's collectives and lax.ppermute only.
A program may use at most 64 MiB of HBM per device.

v0:
```python
import jax
import jax.numpy as jnp
from jax import lax
from jax.sharding import PartitionSpec as P

TGT = 128
TURNS = 2


ridge_weight = 0.5


def passed_along(block, axis, distance):
    devices = range(lax.axis_size(axis))
    route = [((i - distance) % len(devices), i) for i in devices]
    return lax.ppermute(block, axis, route)


def local(features, inverse_gram, targets):
    block_count = lax.axis_size("feat")
    position = lax.axis_index("feat")
    panel_width = targets.shape[0]

    def refine(panel_rows, panel_weights):
        partial_value = jnp.dot(
            panel_rows.astype(jnp.bfloat16), features, preferred_element_type=jnp.float32
        )
        projection = lax.psum(partial_value, "rows")
        increment = jnp.dot(
            projection - ridge_weight * panel_weights, inverse_gram, precision=lax.Precision.HIGHEST
        )
        fitted = lax.dot_general(
            increment.astype(jnp.bfloat16),
            features,
            (((1,), (1,)), ((), ())),
            preferred_element_type=jnp.float32,
        )
        return (panel_rows - fitted, panel_weights + increment)

    def advance(section, carried):
        residual, weights = carried
        panel_index = (position - section) % block_count
        start = panel_index * panel_width
        panel_weights = lax.dynamic_slice_in_dim(weights, start, panel_width, 0)
        residual, panel_weights = refine(residual, panel_weights)
        weights = lax.dynamic_update_slice_in_dim(weights, panel_weights, start, 0)
        residual = passed_along(residual, "feat", 1)
        return (residual, weights)

    carried = (targets, jnp.zeros((TGT, features.shape[1]), jnp.float32))
    for sweep_index in range(TURNS):
        offset = sweep_index * block_count

        def sweep_step(inner, state, offset=offset):
            return advance(inner + offset, state)

        carried = lax.fori_loop(0, block_count, sweep_step, carried)
    residual, weights = carried
    return (weights, residual)


def solution(mesh):
    placed = (P("rows", "feat"), P("feat", None), P("feat", "rows"))
    return jax.shard_map(
        local,
        mesh=mesh,
        in_specs=placed,
        out_specs=(P(None, "feat"), P("feat", "rows")),
        check_vma=False,
    )
```

profile of v0, /device:TPU:1, one launch (start us, length us, event | category | flops | bytes accessed | tf_op | source)
XLA Modules:
  0.0 1923.9 jit_solution(16532286769631520528)
XLA Ops:
  1.4 961.8 %while.34 = (s32[]{:T(128)}, f32[8,1024]{1,0:T(8,128)S(1)}, f32[128,1024]{1,0:T(8,128)S(1)}, bf16[1024,1024]{1,0:T(8,128)(2,1)}, s32[]{:T(128)}, /*index=5*/f32[...) while((s32[]{:T(128)}, f32[8,1024]{1,0:T(8,128)S(1)}, ...), condition=%wide.region_2.3_spmd, body=%wide.region_0.2_spmd.sunk | while | flops 134275072 | bytes 17334632 | solution.py:57
  3.4 48.8 %psum.30 = f32[8,1024]{1,0:T(8,128)S(1)} all-reduce(f32[8,1024]{1,0:T(8,128)S(1)} %fusion.48), channel_id=1, replica_groups=mesh['rows'=16,'feat'=16] {'rows'}, use_global_device_ids=true, to_apply=%region_1.1 | all-reduce | flops 8192 | bytes 65536 | tf_op jit(solution)/shard_map/while/body/eval_jaxpr/psum | solution.py:28
  125.4 46.9 %psum.30 = f32[8,1024]{1,0:T(8,128)S(1)} all-reduce(f32[8,1024]{1,0:T(8,128)S(1)} %fusion.48), channel_id=1, replica_groups=mesh['rows'=16,'feat'=16] {'rows'}, use_global_device_ids=true, to_apply=%region_1.1 | all-reduce | flops 8192 | bytes 65536 | tf_op jit(solution)/shard_map/while/body/eval_jaxpr/psum | solution.py:28
  185.4 46.9 %psum.30 = f32[8,1024]{1,0:T(8,128)S(1)} all-reduce(f32[8,1024]{1,0:T(8,128)S(1)} %fusion.48), channel_id=1, replica_groups=mesh['rows'=16,'feat'=16] {'rows'}, use_global_device_ids=true, to_apply=%region_1.1 | all-reduce | flops 8192 | bytes 65536 | tf_op jit(solution)/shard_map/while/body/eval_jaxpr/psum | solution.py:28
  245.4 46.9 %psum.30 = f32[8,1024]{1,0:T(8,128)S(1)} all-reduce(f32[8,1024]{1,0:T(8,128)S(1)} %fusion.48), channel_id=1, replica_groups=mesh['rows'=16,'feat'=16] {'rows'}, use_global_device_ids=true, to_apply=%region_1.1 | all-reduce | flops 8192 | bytes 65536 | tf_op jit(solution)/shard_map/while/body/eval_jaxpr/psum | solution.py:28
  305.3 46.9 %psum.30 = f32[8,1024]{1,0:T(8,128)S(1)} all-reduce(f32[8,1024]{1,0:T(8,128)S(1)} %fusion.48), channel_id=1, replica_groups=mesh['rows'=16,'feat'=16] {'rows'}, use_global_device_ids=true, to_apply=%region_1.1 | all-reduce | flops 8192 | bytes 65536 | tf_op jit(solution)/shard_map/while/body/eval_jaxpr/psum | solution.py:28
  365.3 46.9 %psum.30 = f32[8,1024]{1,0:T(8,128)S(1)} all-reduce(f32[8,1024]{1,0:T(8,128)S(1)} %fusion.48), channel_id=1, replica_groups=mesh['rows'=16,'feat'=16] {'rows'}, use_global_device_ids=true, to_apply=%region_1.1 | all-reduce | flops 8192 | bytes 65536 | tf_op jit(solution)/shard_map/while/body/eval_jaxpr/psum | solution.py:28
  425.3 46.9 %psum.30 = f32[8,1024]{1,0:T(8,128)S(1)} all-reduce(f32[8,1024]{1,0:T(8,128)S(1)} %fusion.48), channel_id=1, replica_groups=mesh['rows'=16,'feat'=16] {'rows'}, use_global_device_ids=true, to_apply=%region_1.1 | all-reduce | flops 8192 | bytes 65536 | tf_op jit(solution)/shard_map/while/body/eval_jaxpr/psum | solution.py:28
  485.3 46.9 %psum.30 = f32[8,1024]{1,0:T(8,128)S(1)} all-reduce(f32[8,1024]{1,0:T(8,128)S(1)} %fusion.48), channel_id=1, replica_groups=mesh['rows'=16,'feat'=16] {'rows'}, use_global_device_ids=true, to_apply=%region_1.1 | all-reduce | flops 8192 | bytes 65536 | tf_op jit(solution)/shard_map/while/body/eval_jaxpr/psum | solution.py:28
  545.3 46.9 %psum.30 = f32[8,1024]{1,0:T(8,128)S(1)} all-reduce(f32[8,1024]{1,0:T(8,128)S(1)} %fusion.48), channel_id=1, replica_groups=mesh['rows'=16,'feat'=16] {'rows'}, use_global_device_ids=true, to_apply=%region_1.1 | all-reduce | flops 8192 | bytes 65536 | tf_op jit(solution)/shard_map/while/body/eval_jaxpr/psum | solution.py:28
  605.3 46.9 %psum.30 = f32[8,1024]{1,0:T(8,128)S(1)} all-reduce(f32[8,1024]{1,0:T(8,128)S(1)} %fusion.48), channel_id=1, replica_groups=mesh['rows'=16,'feat'=16] {'rows'}, use_global_device_ids=true, to_apply=%region_1.1 | all-reduce | flops 8192 | bytes 65536 | tf_op jit(solution)/shard_map/while/body/eval_jaxpr/psum | solution.py:28
  665.3 46.9 %psum.30 = f32[8,1024]{1,0:T(8,128)S(1)} all-reduce(f32[8,1024]{1,0:T(8,128)S(1)} %fusion.48), channel_id=1, replica_groups=mesh['rows'=16,'feat'=16] {'rows'}, use_global_device_ids=true, to_apply=%region_1.1 | all-reduce | flops 8192 | bytes 65536 | tf_op jit(solution)/shard_map/while/body/eval_jaxpr/psum | solution.py:28
  725.3 46.9 %psum.30 = f32[8,1024]{1,0:T(8,128)S(1)} all-reduce(f32[8,1024]{1,0:T(8,128)S(1)} %fusion.48), channel_id=1, replica_groups=mesh['rows'=16,'feat'=16] {'rows'}, use_global_device_ids=true, to_apply=%region_1.1 | all-reduce | flops 8192 | bytes 65536 | tf_op jit(solution)/shard_map/while/body/eval_jaxpr/psum | solution.py:28
  785.3 46.9 %psum.30 = f32[8,1024]{1,0:T(8,128)S(1)} all-reduce(f32[8,1024]{1,0:T(8,128)S(1)} %fusion.48), channel_id=1, replica_groups=mesh['rows'=16,'feat'=16] {'rows'}, use_global_device_ids=true, to_apply=%region_1.1 | all-reduce | flops 8192 | bytes 65536 | tf_op jit(solution)/shard_map/while/body/eval_jaxpr/psum | solution.py:28
  845.3 46.9 %psum.30 = f32[8,1024]{1,0:T(8,128)S(1)} all-reduce(f32[8,1024]{1,0:T(8,128)S(1)} %fusion.48), channel_id=1, replica_groups=mesh['rows'=16,'feat'=16] {'rows'}, use_global_device_ids=true, to_apply=%region_1.1 | all-reduce | flops 8192 | bytes 65536 | tf_op jit(solution)/shard_map/while/body/eval_jaxpr/psum | solution.py:28
  905.2 46.9 %psum.30 = f32[8,1024]{1,0:T(8,128)S(1)} all-reduce(f32[8,1024]{1,0:T(8,128)S(1)} %fusion.48), channel_id=1, replica_groups=mesh['rows'=16,'feat'=16] {'rows'}, use_global_device_ids=true, to_apply=%region_1.1 | all-reduce | flops 8192 | bytes 65536 | tf_op jit(solution)/shard_map/while/body/eval_jaxpr/psum | solution.py:28
  963.3 959.8 %while.35 = (s32[]{:T(128)}, f32[8,1024]{1,0:T(8,128)S(1)}, f32[128,1024]{1,0:T(8,128)S(1)}, bf16[1024,1024]{1,0:T(8,128)(2,1)}, s32[]{:T(128)}, /*index=5*/f32[...) while((s32[]{:T(128)}, f32[8,1024]{1,0:T(8,128)S(1)}, ...), condition=%wide.region_5.6_spmd, body=%wide.region_3.5_spmd.sunk | while | flops 134275072 | bytes 17334644 | solution.py:57
  965.2 46.9 %psum.31 = f32[8,1024]{1,0:T(8,128)S(1)} all-reduce(f32[8,1024]{1,0:T(8,128)S(1)} %fusion.56), channel_id=1, replica_groups=mesh['rows'=16,'feat'=16] {'rows'}, use_global_device_ids=true, to_apply=%region_4.4 | all-reduce | flops 8192 | bytes 65536 | tf_op jit(solution)/shard_map/while/body/eval_jaxpr/psum | solution.py:28
  1025.2 46.9 %psum.31 = f32[8,1024]{1,0:T(8,128)S(1)} all-reduce(f32[8,1024]{1,0:T(8,128)S(1)} %fusion.56), channel_id=1, replica_groups=mesh['rows'=16,'feat'=16] {'rows'}, use_global_device_ids=true, to_apply=%region_4.4 | all-reduce | flops 8192 | bytes 65536 | tf_op jit(solution)/shard_map/while/body/eval_jaxpr/psum | solution.py:28
  1085.2 46.9 %psum.31 = f32[8,1024]{1,0:T(8,128)S(1)} all-reduce(f32[8,1024]{1,0:T(8,128)S(1)} %fusion.56), channel_id=1, replica_groups=mesh['rows'=16,'feat'=16] {'rows'}, use_global_device_ids=true, to_apply=%region_4.4 | all-reduce | flops 8192 | bytes 65536 | tf_op jit(solution)/shard_map/while/body/eval_jaxpr/psum | solution.py:28
  1145.2 46.9 %psum.31 = f32[8,1024]{1,0:T(8,128)S(1)} all-reduce(f32[8,1024]{1,0:T(8,128)S(1)} %fusion.56), channel_id=1, replica_groups=mesh['rows'=16,'feat'=16] {'rows'}, use_global_device_ids=true, to_apply=%region_4.4 | all-reduce | flops 8192 | bytes 65536 | tf_op jit(solution)/shard_map/while/body/eval_jaxpr/psum | solution.py:28
  1205.2 46.9 %psum.31 = f32[8,1024]{1,0:T(8,128)S(1)} all-reduce(f32[8,1024]{1,0:T(8,128)S(1)} %fusion.56), channel_id=1, replica_groups=mesh['rows'=16,'feat'=16] {'rows'}, use_global_device_ids=true, to_apply=%region_4.4 | all-reduce | flops 8192 | bytes 65536 | tf_op jit(solution)/shard_map/while/body/eval_jaxpr/psum | solution.py:28
  1265.2 46.9 %psum.31 = f32[8,1024]{1,0:T(8,128)S(1)} all-reduce(f32[8,1024]{1,0:T(8,128)S(1)} %fusion.56), channel_id=1, replica_groups=mesh['rows'=16,'feat'=16] {'rows'}, use_global_device_ids=true, to_apply=%region_4.4 | all-reduce | flops 8192 | bytes 65536 | tf_op jit(solution)/shard_map/while/body/eval_jaxpr/psum | solution.py:28
  1325.2 46.9 %psum.31 = f32[8,1024]{1,0:T(8,128)S(1)} all-reduce(f32[8,1024]{1,0:T(8,128)S(1)} %fusion.56), channel_id=1, replica_groups=mesh['rows'=16,'feat'=16] {'rows'}, use_global_device_ids=true, to_apply=%region_4.4 | all-reduce | flops 8192 | bytes 65536 | tf_op jit(solution)/shard_map/while/body/eval_jaxpr/psum | solution.py:28
  1385.2 46.9 %psum.31 = f32[8,1024]{1,0:T(8,128)S(1)} all-reduce(f32[8,1024]{1,0:T(8,128)S(1)} %fusion.56), channel_id=1, replica_groups=mesh['rows'=16,'feat'=16] {'rows'}, use_global_device_ids=true, to_apply=%region_4.4 | all-reduce | flops 8192 | bytes 65536 | tf_op jit(solution)/shard_map/while/body/eval_jaxpr/psum | solution.py:28
  1445.2 46.9 %psum.31 = f32[8,1024]{1,0:T(8,128)S(1)} all-reduce(f32[8,1024]{1,0:T(8,128)S(1)} %fusion.56), channel_id=1, replica_groups=mesh['rows'=16,'feat'=16] {'rows'}, use_global_device_ids=true, to_apply=%region_4.4 | all-reduce | flops 8192 | bytes 65536 | tf_op jit(solution)/shard_map/while/body/eval_jaxpr/psum | solution.py:28
  1505.1 46.9 %psum.31 = f32[8,1024]{1,0:T(8,128)S(1)} all-reduce(f32[8,1024]{1,0:T(8,128)S(1)} %fusion.56), channel_id=1, replica_groups=mesh['rows'=16,'feat'=16] {'rows'}, use_global_device_ids=true, to_apply=%region_4.4 | all-reduce | flops 8192 | bytes 65536 | tf_op jit(solution)/shard_map/while/body/eval_jaxpr/psum | solution.py:28
  1565.1 46.9 %psum.31 = f32[8,1024]{1,0:T(8,128)S(1)} all-reduce(f32[8,1024]{1,0:T(8,128)S(1)} %fusion.56), channel_id=1, replica_groups=mesh['rows'=16,'feat'=16] {'rows'}, use_global_device_ids=true, to_apply=%region_4.4 | all-reduce | flops 8192 | bytes 65536 | tf_op jit(solution)/shard_map/while/body/eval_jaxpr/psum | solution.py:28
  1625.1 46.9 %psum.31 = f32[8,1024]{1,0:T(8,128)S(1)} all-reduce(f32[8,1024]{1,0:T(8,128)S(1)} %fusion.56), channel_id=1, replica_groups=mesh['rows'=16,'feat'=16] {'rows'}, use_global_device_ids=true, to_apply=%region_4.4 | all-reduce | flops 8192 | bytes 65536 | tf_op jit(solution)/shard_map/while/body/eval_jaxpr/psum | solution.py:28
  1685.1 46.9 %psum.31 = f32[8,1024]{1,0:T(8,128)S(1)} all-reduce(f32[8,1024]{1,0:T(8,128)S(1)} %fusion.56), channel_id=1, replica_groups=mesh['rows'=16,'feat'=16] {'rows'}, use_global_device_ids=true, to_apply=%region_4.4 | all-reduce | flops 8192 | bytes 65536 | tf_op jit(solution)/shard_map/while/body/eval_jaxpr/psum | solution.py:28
  1745.1 46.9 %psum.31 = f32[8,1024]{1,0:T(8,128)S(1)} all-reduce(f32[8,1024]{1,0:T(8,128)S(1)} %fusion.56), channel_id=1, replica_groups=mesh['rows'=16,'feat'=16] {'rows'}, use_global_device_ids=true, to_apply=%region_4.4 | all-reduce | flops 8192 | bytes 65536 | tf_op jit(solution)/shard_map/while/body/eval_jaxpr/psum | solution.py:28
  1805.1 46.9 %psum.31 = f32[8,1024]{1,0:T(8,128)S(1)} all-reduce(f32[8,1024]{1,0:T(8,128)S(1)} %fusion.56), channel_id=1, replica_groups=mesh['rows'=16,'feat'=16] {'rows'}, use_global_device_ids=true, to_apply=%region_4.4 | all-reduce | flops 8192 | bytes 65536 | tf_op jit(solution)/shard_map/while/body/eval_jaxpr/psum | solution.py:28
  (263 shorter events, 515.2 us)
Async XLA Ops:
  57.3 6.2 collective-permute-start
  117.3 6.1 collective-permute-start
  177.3 6.1 collective-permute-start
  237.3 6.1 collective-permute-start
  297.3 6.1 collective-permute-start
  357.3 6.1 collective-permute-start
  417.3 6.1 collective-permute-start
  477.2 6.1 collective-permute-start
  537.2 6.1 collective-permute-start
  597.2 6.1 collective-permute-start
  657.2 6.1 collective-permute-start
  717.2 6.1 collective-permute-start
  777.2 6.1 collective-permute-start
  837.2 6.1 collective-permute-start
  897.2 6.1 collective-permute-start
  957.2 6.1 collective-permute-start
  1017.1 6.1 collective-permute-start.1
  1077.1 6.1 collective-permute-start.1
  1137.1 6.1 collective-permute-start.1
  1197.1 6.1 collective-permute-start.1
  1257.1 6.1 collective-permute-start.1
  1317.1 6.1 collective-permute-start.1
  1377.1 6.1 collective-permute-start.1
  1437.1 6.1 collective-permute-start.1
  1497.1 6.1 collective-permute-start.1
  1557.1 6.1 collective-permute-start.1
  1617.0 6.1 collective-permute-start.1
  1677.0 6.1 collective-permute-start.1
  1737.0 6.1 collective-permute-start.1
  1797.0 6.1 collective-permute-start.1
  1857.0 6.1 collective-permute-start.1
  1917.0 6.1 collective-permute-start.1
  (33 other events, 142.2 us)
where the time goes:
time: 1930 us; the launch traced here: 1920 us
  blocking collectives  1500 us (78%)
  matrix products  225 us (12%)
  waiting for transfers between devices  193 us (10%)
    psum x32, blocking collectives, refine(): projection = lax.psum(partial_value, 'rows')  1500 us
    ppermute x32, waiting for transfers between devices, passed_along(): return lax.ppermute(block, axis, route)  193 us
    dot_general x32, matrix products, refine(): jnp.dot(projection - ridge_weight * panel_weights, inverse_gram, precisio...  141 us
    dot_general x32, matrix products, refine(): jnp.dot(panel_rows.astype(jnp.bfloat16), features, preferred_element_type...  63.1 us
  transfers between devices with their start and end apart: 32, of which 32 were waited for; matrix products, arithmetic and copies ran while one was open for 0% of the time, Pallas kernels for 0%

commit v1 on v0

v1 whole, which is shorter than its diff:
```python
import jax
import jax.numpy as jnp
from jax import lax
from jax.sharding import Mesh, PartitionSpec as P

TGT = 128
TURNS = 2
HALF = 2

ridge_weight = 0.5
BF = jnp.bfloat16
F32 = jnp.float32


def passed_along(block, axes, count, distance):
    route = [(i, (i + distance) % count) for i in range(count)]
    return lax.ppermute(block, axes, route)


def dot(a, b, dims=(((1,), (0,)), ((), ()))):
    return lax.dot_general(a, b, dims, preferred_element_type=F32)


def split_dot(a, b):
    high = b.astype(BF)
    low = (b - high.astype(F32)).astype(BF)
    return dot(a, high) + dot(a, low)


def local(features, inverse_gram, targets):
    block_count = lax.axis_size("x") * lax.axis_size("y")
    depth = lax.axis_size("z")
    position = lax.axis_index(("x", "y"))
    core = lax.axis_index("core")
    width = targets.shape[0]
    rows, columns = features.shape
    half = columns // HALF

    one = 1.0 + jnp.minimum(core, 0).astype(F32)

    def other_core(block):
        return passed_along(block, "core", HALF, 1) * one

    def in_order(mine, theirs, dim):
        first = jnp.where(core == 0, mine, theirs)
        second = jnp.where(core == 0, theirs, mine)
        return jnp.concatenate([first, second], dim)

    def half_of(block, which):
        return lax.dynamic_slice_in_dim(block, which * half, half, 1)

    gained = split_dot(features, inverse_gram)
    own_z = half_of(features, core)
    own_h = half_of(gained, core)
    sent_z = half_of(features, 1 - core).astype(F32)
    sent_h = half_of(gained, 1 - core)
    chip_z = in_order(own_z, other_core(sent_z).astype(BF), 0)
    chip_h = in_order(own_h.astype(BF), other_core(sent_h).astype(BF), 0)
    residual = in_order(targets, other_core(targets), 1)

    def section(residual, ridge_term):
        part = dot(residual.astype(BF), chip_h)
        parts = lax.all_to_all(jnp.broadcast_to(part[None], (depth, width, half)), "z", 0, 0)
        increment = jnp.sum(parts, 0)
        if ridge_term is not None:
            increment = increment - ridge_term
        update = dot(increment.astype(BF), chip_z, (((1,), (1,)), ((), ())))
        residual = residual - in_sum(update)
        residual = passed_along(residual, ("x", "y"), block_count, 1)
        return residual, increment

    def in_sum(update):
        return update + passed_along(update, "core", HALF, 1)

    def first_turn(step, carried):
        residual, kept_weights = carried
        residual, increment = section(residual, None)
        return residual, lax.dynamic_update_slice_in_dim(kept_weights, increment[None], step, 0)

    weights = jnp.zeros((block_count, width, half), F32)
    residual, weights = lax.fori_loop(0, block_count, first_turn, (residual, weights))
    flat = weights.reshape(block_count * width, half)
    whole = in_order(flat, passed_along(flat, "core", HALF, 1), 1)
    ridge_terms = ridge_weight * jnp.dot(
        whole, half_of(inverse_gram, core), precision=lax.Precision.HIGHEST
    )
    ridge_terms = ridge_terms.reshape(block_count, width, half)

    def second_turn(step, carried):
        residual, kept_weights = carried
        term = lax.dynamic_index_in_dim(ridge_terms, step, 0, False)
        old = lax.dynamic_index_in_dim(kept_weights, step, 0, False)
        residual, increment = section(residual, term)
        return residual, lax.dynamic_update_slice_in_dim(
            kept_weights, (old + increment)[None], step, 0
        )

    residual, weights = lax.fori_loop(0, block_count, second_turn, (residual, weights))

    order = (position - jnp.arange(block_count)) % block_count
    weights = weights[order].reshape(block_count * width, half)
    weights = in_order(weights, passed_along(weights, "core", HALF, 1), 1)
    return weights, lax.dynamic_slice_in_dim(residual, core * rows, rows, 1)


def solution(mesh):
    inner = Mesh(mesh.devices.reshape(-1, HALF, 4, 4), ("z", "core", "x", "y"))
    rows, feat = ("z", "core"), ("x", "y")
    return jax.shard_map(
        local,
        mesh=inner,
        in_specs=(P(rows, feat), P(feat, None), P(feat, rows)),
        out_specs=(P(None, feat), P(feat, rows)),
        check_vma=False,
    )
```

time: 1930 us -> 808 us (0.42)
  blocking collectives: 1500 us -> 169 us
  waiting for transfers between devices: 193 us -> 366 us
  starting transfers between devices: 1.39 us -> 148 us
  matrix products: 225 us -> 95.6 us
    psum x32 -> x0, blocking collectives: 1500 us -> none  [refine(): projection = lax.psum(partial_value, 'rows')]
    all_to_all x0 -> x16, blocking collectives: none -> 169 us  [section(): lax.all_to_all(jnp.broadcast_to(part[None], (depth, width, half)), 'z', 0...]
    dot_general x96 -> x67, matrix products: 225 us -> 95.6 us  [the longest x66 92.8 us: dot(): return lax.dot_general(a, b, dims, preferred_element_type=F32)]
    all_to_all x0 -> x16, waiting for transfers between devices: none -> 126 us  [section(): lax.all_to_all(jnp.broadcast_to(part[None], (depth, width, half)), 'z', 0...]
    ppermute x32 -> x69, starting transfers between devices: 1.39 us -> 94 us  [passed_along(): return lax.ppermute(block, axes, route)]
    all_to_all x0 -> x16, starting transfers between devices: none -> 54 us  [section(): lax.all_to_all(jnp.broadcast_to(part[None], (depth, width, half)), 'z', 0...]
    ppermute x32 -> x69, waiting for transfers between devices: 193 us -> 240 us  [passed_along(): return lax.ppermute(block, axes, route)]
  transfers between devices with their start and end apart: 32 -> 85, of which waited for: 32 -> 83; matrix products, arithmetic and copies ran while one was open for 0% -> 1% of each run, Pallas kernels for 0% -> 0%
where the time goes in v1:
time: 808 us; the launch traced here: 804 us
  waiting for transfers between devices  366 us (45%)
  blocking collectives  169 us (21%)
  starting transfers between devices  148 us (18%)
  matrix products  95.6 us (12%)
  local copies, waits for them, and re-layouts  15.7 us (2%)
  other arithmetic  8.55 us (1%)
    ppermute x69, waiting for transfers between devices, passed_along(): return lax.ppermute(block, axes, route)  240 us
    all_to_all x16, blocking collectives, section(): lax.all_to_all(jnp.broadcast_to(part[None], (depth, width, half)), 'z', 0...  169 us
    all_to_all x16, waiting for transfers between devices, section(): lax.all_to_all(jnp.broadcast_to(part[None], (depth, width, half)), 'z', 0...  126 us
    ppermute x69, starting transfers between devices, passed_along(): return lax.ppermute(block, axes, route)  94 us
    dot_general x66, matrix products, dot(): return lax.dot_general(a, b, dims, preferred_element_type=F32)  92.8 us
    all_to_all x16, starting transfers between devices, section(): lax.all_to_all(jnp.broadcast_to(part[None], (depth, width, half)), 'z', 0...  54 us
  transfers between devices with their start and end apart: 85, of which 83 were waited for; matrix products, arithmetic and copies ran while one was open for 1% of the time, Pallas kernels for 0%

profile of v1, /device:TPU:1, one launch (start us, length us, event | category | flops | bytes accessed | tf_op | source)
XLA Modules:
  0.0 804.4 jit_solution(9263475391724700271)
XLA Ops:
  28.8 372.3 %while.30 = (s32[]{:T(128)}, f32[8,2048]{1,0:T(8,128)S(1)}, f32[16,8,512]{2,1,0:T(8,128)S(1)}, bf16[2048,512]{1,0:T(8,128)(2,1)S(1)}, bf16[2048,512]{1,0:T(8,128)(2,1)}, /*index=5*/s32[]{:T(128)}, f32[]{:T(128)}) while((s32[]{:T(128)}, f32[8,2048]{1,0:T(8,128)S(1)}, f32[16,8,512]{2,1,0:T(8,128)S(1)}, bf16[2048,512]{1,0:T(8,128)(2,1)S(1)}, ...), condition=%wide.region_2.3_spmd, body=%wide.region_0.2_spmd.sunk | while | flops 33636352 | bytes 5734573 | solution.py:81
  29.2 14.0 %all_to_all.20 = f32[8,8,512]{2,1,0:T(8,128)S(1)} all-to-all(f32[8,8,512]{2,1,0:T(8,128)S(1)} %broadcast_in_dim.49), channel_id=1, replica_groups=mesh['z'=8,'core'=2,'x'=4,'y'=4] {'z'}, dimensions={0} | all-to-all | bytes 262144 | tf_op jit(solution)/shard_map/while/body/eval_jaxpr/all_to_all | solution.py:63
  56.0 10.1 %all_to_all.20 = f32[8,8,512]{2,1,0:T(8,128)S(1)} all-to-all(f32[8,8,512]{2,1,0:T(8,128)S(1)} %broadcast_in_dim.49), channel_id=1, replica_groups=mesh['z'=8,'core'=2,'x'=4,'y'=4] {'z'}, dimensions={0} | all-to-all | bytes 262144 | tf_op jit(solution)/shard_map/while/body/eval_jaxpr/all_to_all | solution.py:63
  78.6 10.3 %all_to_all.20 = f32[8,8,512]{2,1,0:T(8,128)S(1)} all-to-all(f32[8,8,512]{2,1,0:T(8,128)S(1)} %broadcast_in_dim.49), channel_id=1, replica_groups=mesh['z'=8,'core'=2,'x'=4,'y'=4] {'z'}, dimensions={0} | all-to-all | bytes 262144 | tf_op jit(solution)/shard_map/while/body/eval_jaxpr/all_to_all | solution.py:63
  101.7 10.3 %all_to_all.20 = f32[8,8,512]{2,1,0:T(8,128)S(1)} all-to-all(f32[8,8,512]{2,1,0:T(8,128)S(1)} %broadcast_in_dim.49), channel_id=1, replica_groups=mesh['z'=8,'core'=2,'x'=4,'y'=4] {'z'}, dimensions={0} | all-to-all | bytes 262144 | tf_op jit(solution)/shard_map/while/body/eval_jaxpr/all_to_all | solution.py:63
  124.8 10.3 %all_to_all.20 = f32[8,8,512]{2,1,0:T(8,128)S(1)} all-to-all(f32[8,8,512]{2,1,0:T(8,128)S(1)} %broadcast_in_dim.49), channel_id=1, replica_groups=mesh['z'=8,'core'=2,'x'=4,'y'=4] {'z'}, dimensions={0} | all-to-all | bytes 262144 | tf_op jit(solution)/shard_map/while/body/eval_jaxpr/all_to_all | solution.py:63
  147.8 10.3 %all_to_all.20 = f32[8,8,512]{2,1,0:T(8,128)S(1)} all-to-all(f32[8,8,512]{2,1,0:T(8,128)S(1)} %broadcast_in_dim.49), channel_id=1, replica_groups=mesh['z'=8,'core'=2,'x'=4,'y'=4] {'z'}, dimensions={0} | all-to-all | bytes 262144 | tf_op jit(solution)/shard_map/while/body/eval_jaxpr/all_to_all | solution.py:63
  170.9 10.3 %all_to_all.20 = f32[8,8,512]{2,1,0:T(8,128)S(1)} all-to-all(f32[8,8,512]{2,1,0:T(8,128)S(1)} %broadcast_in_dim.49), channel_id=1, replica_groups=mesh['z'=8,'core'=2,'x'=4,'y'=4] {'z'}, dimensions={0} | all-to-all | bytes 262144 | tf_op jit(solution)/shard_map/while/body/eval_jaxpr/all_to_all | solution.py:63
  193.9 10.3 %all_to_all.20 = f32[8,8,512]{2,1,0:T(8,128)S(1)} all-to-all(f32[8,8,512]{2,1,0:T(8,128)S(1)} %broadcast_in_dim.49), channel_id=1, replica_groups=mesh['z'=8,'core'=2,'x'=4,'y'=4] {'z'}, dimensions={0} | all-to-all | bytes 262144 | tf_op jit(solution)/shard_map/while/body/eval_jaxpr/all_to_all | solution.py:63
  217.0 10.3 %all_to_all.20 = f32[8,8,512]{2,1,0:T(8,128)S(1)} all-to-all(f32[8,8,512]{2,1,0:T(8,128)S(1)} %broadcast_in_dim.49), channel_id=1, replica_groups=mesh['z'=8,'core'=2,'x'=4,'y'=4] {'z'}, dimensions={0} | all-to-all | bytes 262144 | tf_op jit(solution)/shard_map/while/body/eval_jaxpr/all_to_all | solution.py:63
  240.0 10.3 %all_to_all.20 = f32[8,8,512]{2,1,0:T(8,128)S(1)} all-to-all(f32[8,8,512]{2,1,0:T(8,128)S(1)} %broadcast_in_dim.49), channel_id=1, replica_groups=mesh['z'=8,'core'=2,'x'=4,'y'=4] {'z'}, dimensions={0} | all-to-all | bytes 262144 | tf_op jit(solution)/shard_map/while/body/eval_jaxpr/all_to_all | solution.py:63
  263.1 10.3 %all_to_all.20 = f32[8,8,512]{2,1,0:T(8,128)S(1)} all-to-all(f32[8,8,512]{2,1,0:T(8,128)S(1)} %broadcast_in_dim.49), channel_id=1, replica_groups=mesh['z'=8,'core'=2,'x'=4,'y'=4] {'z'}, dimensions={0} | all-to-all | bytes 262144 | tf_op jit(solution)/shard_map/while/body/eval_jaxpr/all_to_all | solution.py:63
  286.1 10.3 %all_to_all.20 = f32[8,8,512]{2,1,0:T(8,128)S(1)} all-to-all(f32[8,8,512]{2,1,0:T(8,128)S(1)} %broadcast_in_dim.49), channel_id=1, replica_groups=mesh['z'=8,'core'=2,'x'=4,'y'=4] {'z'}, dimensions={0} | all-to-all | bytes 262144 | tf_op jit(solution)/shard_map/while/body/eval_jaxpr/all_to_all | solution.py:63
  309.2 10.3 %all_to_all.20 = f32[8,8,512]{2,1,0:T(8,128)S(1)} all-to-all(f32[8,8,512]{2,1,0:T(8,128)S(1)} %broadcast_in_dim.49), channel_id=1, replica_groups=mesh['z'=8,'core'=2,'x'=4,'y'=4] {'z'}, dimensions={0} | all-to-all | bytes 262144 | tf_op jit(solution)/shard_map/while/body/eval_jaxpr/all_to_all | solution.py:63
  332.3 10.3 %all_to_all.20 = f32[8,8,512]{2,1,0:T(8,128)S(1)} all-to-all(f32[8,8,512]{2,1,0:T(8,128)S(1)} %broadcast_in_dim.49), channel_id=1, replica_groups=mesh['z'=8,'core'=2,'x'=4,'y'=4] {'z'}, dimensions={0} | all-to-all | bytes 262144 | tf_op jit(solution)/shard_map/while/body/eval_jaxpr/all_to_all | solution.py:63
  355.3 10.3 %all_to_all.20 = f32[8,8,512]{2,1,0:T(8,128)S(1)} all-to-all(f32[8,8,512]{2,1,0:T(8,128)S(1)} %broadcast_in_dim.49), channel_id=1, replica_groups=mesh['z'=8,'core'=2,'x'=4,'y'=4] {'z'}, dimensions={0} | all-to-all | bytes 262144 | tf_op jit(solution)/shard_map/while/body/eval_jaxpr/all_to_all | solution.py:63
  378.4 10.3 %all_to_all.20 = f32[8,8,512]{2,1,0:T(8,128)S(1)} all-to-all(f32[8,8,512]{2,1,0:T(8,128)S(1)} %broadcast_in_dim.49), channel_id=1, replica_groups=mesh['z'=8,'core'=2,'x'=4,'y'=4] {'z'}, dimensions={0} | all-to-all | bytes 262144 | tf_op jit(solution)/shard_map/while/body/eval_jaxpr/all_to_all | solution.py:63
  406.6 393.5 %while.31 = (s32[]{:T(128)}, f32[8,2048]{1,0:T(8,128)S(1)}, f32[16,8,512]{2,1,0:T(8,128)S(1)}, bf16[2048,512]{1,0:T(8,128)(2,1)S(1)}, f32[16,8,512]{2,1,0:T(8,12...) while((s32[]{:T(128)}, f32[8,2048]{1,0:T(8,128)S(1)}, f32[16,8,512]{2,1,0:T(8,128)S(1)}, ...), condition=%wide.region_5.6_spmd, body=%wide.region_3.5_spmd.sunk | while | flops 33648640 | bytes 5914841 | solution.py:98
  411.1 8.2 %all-to-all-done.1 = f32[8,8,512]{2,1,0:T(8,128)S(1)} async-done(((f32[8,8,512]{2,1,0:T(8,128)}), f32[8,8,512]{2,1,0:T(8,128)S(1)}, u32[]{:S(2)}, u32[]{:S(2)}) %all-to-all-start.1) | async-done | bytes 131104 | tf_op jit(solution)/shard_map/while/body/eval_jaxpr/all_to_all | solution.py:63
  435.1 7.9 all-to-all-done.1
  459.8 7.9 all-to-all-done.1
  484.4 7.9 all-to-all-done.1
  509.0 7.9 all-to-all-done.1
  533.7 7.9 all-to-all-done.1
  558.3 7.9 all-to-all-done.1
  582.9 7.9 all-to-all-done.1
  607.6 7.9 all-to-all-done.1
  632.2 7.9 all-to-all-done.1
  656.8 7.9 all-to-all-done.1
  681.4 7.9 all-to-all-done.1
  706.1 7.9 all-to-all-done.1
  730.7 7.9 all-to-all-done.1
  (374 shorter events, 523.2 us)
Async XLA Ops:
  13.4 10.3 %collective-permute-start.5 = (f32[1024,512]{1,0:T(8,128)}, f32[1024,512]{1,0:T(8,128)}, u32[]{:S(2)}, u32[]{:S(2)}) collective-permute-start(f32[1024,512]{1,0:T(8,128)} %constant_dynamic-slice_fusion.1), channel_id=1, source_target_pairs={{0,16},{16,0},{1,17},{17,1},{2,18},{18,2},{3,19},{19,3},{4,20},{20... | collective-permute-start | bytes 6291464 | tf_op jit(solution)/shard_map/ppermute | solution.py:17
  18.2 8.5 %collective-permute-start.6 = (f32[1024,512]{1,0:T(8,128)}, f32[1024,512]{1,0:T(8,128)S(1)}, u32[]{:S(2)}, u32[]{:S(2)}) collective-permute-start(f32[1024,512]{1,0:T(8,128)} %dynamic-slice_convert_fusion.1), channel_id=1, source_target_pairs={{0,16},{16,0},{1,17},{17,1},{2,18},{18,2},{3,19},{19,3},{4,20},{20... | collective-permute-start | bytes 6291464 | tf_op jit(solution)/shard_map/ppermute | solution.py:17
  48.6 7.0 collective-permute-start.1
  71.7 6.5 collective-permute-start.1
  94.8 6.5 collective-permute-start.1
  117.8 6.5 collective-permute-start.1
  140.9 6.5 collective-permute-start.1
  164.0 6.5 collective-permute-start.1
  187.0 6.5 collective-permute-start.1
  210.1 6.5 collective-permute-start.1
  233.1 6.5 collective-permute-start.1
  256.2 6.5 collective-permute-start.1
  279.2 6.5 collective-permute-start.1
  302.3 6.5 collective-permute-start.1
  325.4 6.5 collective-permute-start.1
  348.4 6.5 collective-permute-start.1
  407.7 11.5 %all-to-all-start.1 = ((f32[8,8,512]{2,1,0:T(8,128)}), f32[8,8,512]{2,1,0:T(8,128)S(1)}, u32[]{:S(2)}, u32[]{:S(2)}) async-start(f32[8,8,512]{2,1,0:T(8,128)} %broadcast_in_dim.50), calls=%async_computation.1 | async-start | bytes 262144 | tf_op jit(solution)/shard_map/while/body/eval_jaxpr/all_to_all | solution.py:63
  431.8 11.2 %all-to-all-start.1 = ((f32[8,8,512]{2,1,0:T(8,128)}), f32[8,8,512]{2,1,0:T(8,128)S(1)}, u32[]{:S(2)}, u32[]{:S(2)}) async-start(f32[8,8,512]{2,1,0:T(8,128)} %broadcast_in_dim.50), calls=%async_computation.1 | async-start | bytes 262144 | tf_op jit(solution)/shard_map/while/body/eval_jaxpr/all_to_all | solution.py:63
  456.4 11.2 %all-to-all-start.1 = ((f32[8,8,512]{2,1,0:T(8,128)}), f32[8,8,512]{2,1,0:T(8,128)S(1)}, u32[]{:S(2)}, u32[]{:S(2)}) async-start(f32[8,8,512]{2,1,0:T(8,128)} %broadcast_in_dim.50), calls=%async_computation.1 | async-start | bytes 262144 | tf_op jit(solution)/shard_map/while/body/eval_jaxpr/all_to_all | solution.py:63
  481.0 11.2 %all-to-all-start.1 = ((f32[8,8,512]{2,1,0:T(8,128)}), f32[8,8,512]{2,1,0:T(8,128)S(1)}, u32[]{:S(2)}, u32[]{:S(2)}) async-start(f32[8,8,512]{2,1,0:T(8,128)} %broadcast_in_dim.50), calls=%async_computation.1 | async-start | bytes 262144 | tf_op jit(solution)/shard_map/while/body/eval_jaxpr/all_to_all | solution.py:63
  505.7 11.2 %all-to-all-start.1 = ((f32[8,8,512]{2,1,0:T(8,128)}), f32[8,8,512]{2,1,0:T(8,128)S(1)}, u32[]{:S(2)}, u32[]{:S(2)}) async-start(f32[8,8,512]{2,1,0:T(8,128)} %broadcast_in_dim.50), calls=%async_computation.1 | async-start | bytes 262144 | tf_op jit(solution)/shard_map/while/body/eval_jaxpr/all_to_all | solution.py:63
  530.3 11.2 %all-to-all-start.1 = ((f32[8,8,512]{2,1,0:T(8,128)}), f32[8,8,512]{2,1,0:T(8,128)S(1)}, u32[]{:S(2)}, u32[]{:S(2)}) async-start(f32[8,8,512]{2,1,0:T(8,128)} %broadcast_in_dim.50), calls=%async_computation.1 | async-start | bytes 262144 | tf_op jit(solution)/shard_map/while/body/eval_jaxpr/all_to_all | solution.py:63
  554.9 11.2 %all-to-all-start.1 = ((f32[8,8,512]{2,1,0:T(8,128)}), f32[8,8,512]{2,1,0:T(8,128)S(1)}, u32[]{:S(2)}, u32[]{:S(2)}) async-start(f32[8,8,512]{2,1,0:T(8,128)} %broadcast_in_dim.50), calls=%async_computation.1 | async-start | bytes 262144 | tf_op jit(solution)/shard_map/while/body/eval_jaxpr/all_to_all | solution.py:63
  579.5 11.2 %all-to-all-start.1 = ((f32[8,8,512]{2,1,0:T(8,128)}), f32[8,8,512]{2,1,0:T(8,128)S(1)}, u32[]{:S(2)}, u32[]{:S(2)}) async-start(f32[8,8,512]{2,1,0:T(8,128)} %broadcast_in_dim.50), calls=%async_computation.1 | async-start | bytes 262144 | tf_op jit(solution)/shard_map/while/body/eval_jaxpr/all_to_all | solution.py:63
  604.2 11.2 %all-to-all-start.1 = ((f32[8,8,512]{2,1,0:T(8,128)}), f32[8,8,512]{2,1,0:T(8,128)S(1)}, u32[]{:S(2)}, u32[]{:S(2)}) async-start(f32[8,8,512]{2,1,0:T(8,128)} %broadcast_in_dim.50), calls=%async_computation.1 | async-start | bytes 262144 | tf_op jit(solution)/shard_map/while/body/eval_jaxpr/all_to_all | solution.py:63
  628.8 11.2 %all-to-all-start.1 = ((f32[8,8,512]{2,1,0:T(8,128)}), f32[8,8,512]{2,1,0:T(8,128)S(1)}, u32[]{:S(2)}, u32[]{:S(2)}) async-start(f32[8,8,512]{2,1,0:T(8,128)} %broadcast_in_dim.50), calls=%async_computation.1 | async-start | bytes 262144 | tf_op jit(solution)/shard_map/while/body/eval_jaxpr/all_to_all | solution.py:63
  653.4 11.2 %all-to-all-start.1 = ((f32[8,8,512]{2,1,0:T(8,128)}), f32[8,8,512]{2,1,0:T(8,128)S(1)}, u32[]{:S(2)}, u32[]{:S(2)}) async-start(f32[8,8,512]{2,1,0:T(8,128)} %broadcast_in_dim.50), calls=%async_computation.1 | async-start | bytes 262144 | tf_op jit(solution)/shard_map/while/body/eval_jaxpr/all_to_all | solution.py:63
  678.1 11.2 %all-to-all-start.1 = ((f32[8,8,512]{2,1,0:T(8,128)}), f32[8,8,512]{2,1,0:T(8,128)S(1)}, u32[]{:S(2)}, u32[]{:S(2)}) async-start(f32[8,8,512]{2,1,0:T(8,128)} %broadcast_in_dim.50), calls=%async_computation.1 | async-start | bytes 262144 | tf_op jit(solution)/shard_map/while/body/eval_jaxpr/all_to_all | solution.py:63
  702.7 11.2 %all-to-all-start.1 = ((f32[8,8,512]{2,1,0:T(8,128)}), f32[8,8,512]{2,1,0:T(8,128)S(1)}, u32[]{:S(2)}, u32[]{:S(2)}) async-start(f32[8,8,512]{2,1,0:T(8,128)} %broadcast_in_dim.50), calls=%async_computation.1 | async-start | bytes 262144 | tf_op jit(solution)/shard_map/while/body/eval_jaxpr/all_to_all | solution.py:63
  727.3 11.2 %all-to-all-start.1 = ((f32[8,8,512]{2,1,0:T(8,128)}), f32[8,8,512]{2,1,0:T(8,128)S(1)}, u32[]{:S(2)}, u32[]{:S(2)}) async-start(f32[8,8,512]{2,1,0:T(8,128)} %broadcast_in_dim.50), calls=%async_computation.1 | async-start | bytes 262144 | tf_op jit(solution)/shard_map/while/body/eval_jaxpr/all_to_all | solution.py:63
  752.0 11.2 %all-to-all-start.1 = ((f32[8,8,512]{2,1,0:T(8,128)}), f32[8,8,512]{2,1,0:T(8,128)S(1)}, u32[]{:S(2)}, u32[]{:S(2)}) async-start(f32[8,8,512]{2,1,0:T(8,128)} %broadcast_in_dim.50), calls=%async_computation.1 | async-start | bytes 262144 | tf_op jit(solution)/shard_map/while/body/eval_jaxpr/all_to_all | solution.py:63
  776.6 11.2 %all-to-all-start.1 = ((f32[8,8,512]{2,1,0:T(8,128)}), f32[8,8,512]{2,1,0:T(8,128)S(1)}, u32[]{:S(2)}, u32[]{:S(2)}) async-start(f32[8,8,512]{2,1,0:T(8,128)} %broadcast_in_dim.50), calls=%async_computation.1 | async-start | bytes 262144 | tf_op jit(solution)/shard_map/while/body/eval_jaxpr/all_to_all | solution.py:63
  (57 other events, 258.7 us)

commit v2 on v1

v2 whole, which is shorter than its diff:
```python
import jax
import jax.numpy as jnp
from jax import lax
from jax.experimental import pallas as pl
from jax.experimental.pallas import tpu as pltpu
from jax.experimental.layout import Layout, with_layout_constraint
from jax.sharding import Mesh, PartitionSpec as P

TGT = 128
TURNS = 2
HALF = 2

ridge_weight = 0.5
BF = jnp.bfloat16
F32 = jnp.float32


def turned(x):
    return with_layout_constraint(x.T, Layout((0, 1)))


def projected(residual, h, copies, terms=None, at=None, steps=4):
    width, deep = residual.shape
    wide = h.shape[1]
    chunk = deep // steps

    def kernel(at_ref, r_ref, h_ref, *refs):
        term_ref = refs[0] if terms is not None else None
        out_ref, acc_ref = refs[-2:]
        step = pl.program_id(0)

        @pl.when(step == 0)
        def _():
            acc_ref[...] = jnp.zeros_like(acc_ref) if terms is None else -term_ref[0]

        acc_ref[...] += jnp.dot(r_ref[...].astype(BF), h_ref[...], preferred_element_type=F32)

        @pl.when(step == steps - 1)
        def _():
            out_ref[...] = jnp.broadcast_to(acc_ref[...][None], out_ref.shape)

    extra = [] if terms is None else [pl.BlockSpec((1, width, wide), lambda i, at: (at[0], 0, 0))]
    return pl.pallas_call(
        kernel,
        grid_spec=pltpu.PrefetchScalarGridSpec(
            num_scalar_prefetch=1,
            grid=(steps,),
            in_specs=[
                pl.BlockSpec((width, chunk), lambda i, at: (0, i)),
                pl.BlockSpec((chunk, wide), lambda i, at: (i, 0)),
            ] + extra,
            out_specs=pl.BlockSpec((copies, width, wide), lambda i, at: (0, 0, 0)),
            scratch_shapes=[pltpu.VMEM((width, wide), F32)],
        ),
        out_shape=jax.ShapeDtypeStruct((copies, width, wide), F32),
        compiler_params=pltpu.CompilerParams(vmem_limit_bytes=16 << 20),
        cost_estimate=pl.CostEstimate(
            flops=2 * width * deep * wide, bytes_accessed=2 * deep * wide, transcendentals=0
        ),
        name="projected",
    )(at, residual, h, *([] if terms is None else [terms]))


def corrected(parts, zt, steps=4):
    copies, width, wide = parts.shape
    deep = zt.shape[1]
    chunk = deep // steps

    def kernel(parts_ref, z_ref, inc_ref, out_ref, low_ref):
        @pl.when(pl.program_id(0) == 0)
        def _():
            total = parts_ref[0]
            for i in range(1, copies):
                total = total + parts_ref[i]
            inc_ref[...] = total
            low_ref[...] = total.astype(BF)

        out_ref[...] = jnp.dot(low_ref[...], z_ref[...], preferred_element_type=F32)

    whole = pl.BlockSpec((width, wide), lambda i: (0, 0))
    return pl.pallas_call(
        kernel,
        grid=(steps,),
        in_specs=[
            pl.BlockSpec((copies, width, wide), lambda i: (0, 0, 0)),
            pl.BlockSpec((wide, chunk), lambda i: (0, i)),
        ],
        out_specs=[whole, pl.BlockSpec((width, chunk), lambda i: (0, i))],
        out_shape=[
            jax.ShapeDtypeStruct((width, wide), F32),
            jax.ShapeDtypeStruct((width, deep), F32),
        ],
        scratch_shapes=[pltpu.VMEM((width, wide), BF)],
        compiler_params=pltpu.CompilerParams(vmem_limit_bytes=16 << 20),
        cost_estimate=pl.CostEstimate(
            flops=2 * width * deep * wide, bytes_accessed=2 * deep * wide, transcendentals=0
        ),
        name="corrected",
    )(parts, zt)


def passed_along(block, axes, count, distance):
    route = [(i, (i + distance) % count) for i in range(count)]
    return lax.ppermute(block, axes, route)


def dot(a, b, dims=(((1,), (0,)), ((), ()))):
    return lax.dot_general(a, b, dims, preferred_element_type=F32)


def split_dot(a, b):
    high = b.astype(BF)
    low = (b - high.astype(F32)).astype(BF)
    return dot(a, high) + dot(a, low)


def local(features, inverse_gram, targets):
    block_count = lax.axis_size("x") * lax.axis_size("y")
    depth = lax.axis_size("z")
    position = lax.axis_index(("x", "y"))
    core = lax.axis_index("core")
    width = targets.shape[0]
    rows, columns = features.shape
    half = columns // HALF

    one = 1.0 + jnp.minimum(core, 0).astype(F32)

    def other_core(block):
        return passed_along(block, "core", HALF, 1) * one

    def in_order(mine, theirs, dim):
        first = jnp.where(core == 0, mine, theirs)
        second = jnp.where(core == 0, theirs, mine)
        return jnp.concatenate([first, second], dim)

    def half_of(block, which):
        return lax.dynamic_slice_in_dim(block, which * half, half, 1)

    def swapped(block):
        return passed_along(block, "core", HALF, 1)

    residual = in_order(targets, swapped(targets), 1)
    theirs = other_core(features.astype(F32)).astype(BF)
    my_gram = half_of(inverse_gram, core)
    chip_h = in_order(split_dot(features, my_gram), split_dot(theirs, my_gram), 0).astype(BF)
    chip_z = turned(half_of(in_order(features, theirs, 0), core))

    def section(residual, at, terms=None):
        parts = lax.all_to_all(projected(residual, chip_h, depth, terms, at), "z", 0, 0)
        increment, update = corrected(parts, chip_z)
        residual = residual - (update + swapped(update))
        return passed_along(residual, ("x", "y"), block_count, 1), increment

    def turn(residual, made, terms):
        def one_section(step, carried):
            residual, made, at = carried
            residual, increment = section(residual, at, terms)
            return residual, lax.dynamic_update_slice_in_dim(made, increment[None], step, 0), at + 1

        at = jnp.zeros((1,), jnp.int32)
        return lax.fori_loop(0, block_count, one_section, (residual, made, at))[:2]

    residual, weights = turn(residual, jnp.zeros((block_count, width, half), F32), None)
    flat = weights.reshape(block_count * width, half)
    whole = in_order(flat, swapped(flat), 1)
    terms = ridge_weight * jnp.dot(whole, my_gram, precision=lax.Precision.HIGHEST)
    terms = jnp.where(lax.axis_index("z") == 0, terms, 0.0).reshape(block_count, width, half)
    residual, more = turn(residual, jnp.zeros_like(weights), terms)
    weights = weights + more

    order = (position - jnp.arange(block_count)) % block_count
    weights = weights[order].reshape(block_count * width, half)
    weights = in_order(weights, passed_along(weights, "core", HALF, 1), 1)
    return weights, lax.dynamic_slice_in_dim(residual, core * rows, rows, 1)


def solution(mesh):
    inner = Mesh(mesh.devices.reshape(-1, HALF, 4, 4), ("z", "core", "x", "y"))
    rows, feat = ("z", "core"), ("x", "y")
    return jax.shard_map(
        local,
        mesh=inner,
        in_specs=(P(rows, feat), P(feat, None), P(feat, rows)),
        out_specs=(P(None, feat), P(feat, rows)),
        check_vma=False,
    )
```

time: 808 us -> 753 us (0.932)
  blocking collectives: 169 us -> 335 us
  waiting for transfers between devices: 366 us -> 235 us
  matrix products: 95.6 us -> 9.17 us
  starting transfers between devices: 148 us -> 93.1 us
  Pallas kernels: 0 us -> 52.6 us
  other arithmetic: 8.55 us -> 17.5 us
  local copies, waits for them, and re-layouts: 15.7 us -> 7.35 us
    all_to_all x16 -> x32, blocking collectives: 169 us -> 335 us  [section(): lax.all_to_all(projected(residual, chip_h, depth, terms, at), 'z', 0, 0)]
    all_to_all x16 -> x0, waiting for transfers between devices: 126 us -> none  [section(): lax.all_to_all(jnp.broadcast_to(part[None], (depth, width, half)), 'z', 0...]
    dot_general x66 -> x4, matrix products: 92.8 us -> 6.28 us  [dot(): return lax.dot_general(a, b, dims, preferred_element_type=F32)]
    all_to_all x16 -> x0, starting transfers between devices: 54 us -> none  [section(): lax.all_to_all(jnp.broadcast_to(part[None], (depth, width, half)), 'z', 0...]
    pallas_call x0 -> x64, Pallas kernels: none -> 52.6 us  [the longest x32 28.8 us: corrected(): pl.pallas_call(kernel, grid=(steps,), in_specs=[pl.BlockSpec((copies, wid...]
    broadcast_in_dim x32 -> x0, local copies, waits for them, and re-layouts: 11.2 us -> none  [section(): jnp.broadcast_to(part[None], (depth, width, half))]
    ppermute x69 -> x68, waiting for transfers between devices: 240 us -> 235 us  [passed_along(): return lax.ppermute(block, axes, route)]
    ppermute x69 -> x68, starting transfers between devices: 94 us -> 93.1 us  [passed_along(): return lax.ppermute(block, axes, route)]
  transfers between devices with their start and end apart: 85 -> 68, of which waited for: 83 -> 67; matrix products, arithmetic and copies ran while one was open for 1% -> 1% of each run, Pallas kernels for 0% -> 0%
where the time goes in v2:
time: 753 us; the launch traced here: 752 us
  blocking collectives  335 us (44%)
  waiting for transfers between devices  235 us (31%)
  starting transfers between devices  93.1 us (12%)
  Pallas kernels  52.6 us (7%)
  other arithmetic  17.5 us (2%)
  matrix products  9.17 us (1%)
    all_to_all x32, blocking collectives, section(): lax.all_to_all(projected(residual, chip_h, depth, terms, at), 'z', 0, 0)  335 us
    ppermute x68, waiting for transfers between devices, passed_along(): return lax.ppermute(block, axes, route)  235 us
    ppermute x68, starting transfers between devices, passed_along(): return lax.ppermute(block, axes, route)  93.1 us
    pallas_call x32, Pallas kernels, corrected(): pl.pallas_call(kernel, grid=(steps,), in_specs=[pl.BlockSpec((copies, wid...  28.8 us
    pallas_call x32, Pallas kernels, projected(): pl.pallas_call(kernel, grid_spec=pltpu.PrefetchScalarGridSpec(num_scalar_...  23.8 us
  transfers between devices with their start and end apart: 68, of which 67 were waited for; matrix products, arithmetic and copies ran while one was open for 1% of the time, Pallas kernels for 0%

profile of v2, /device:TPU:1, one launch (start us, length us, event | category | flops | bytes accessed | tf_op | source)
XLA Modules:
  0.0 751.6 jit_solution(1668203343693501988)
XLA Ops:
  32.6 356.6 %while.34 = (s32[]{:T(128)}, f32[8,2048]{1,0:T(8,128)S(1)}, f32[16,8,512]{2,1,0:T(8,128)S(1)}, s32[1]{0:T(128)}, bf16[2048,512]{1,0:T(8,128)(2,1)S(1)}, /*index=5*/bf16[512,2048]{1,0:T(8,128)(2,1)}, s32[]{:T(128)}, s32[1]{0:T(128)}) while((s32[]{:T(128)}, f32[8,2048]{1,0:T(8,128)S(1)}, f32[16,8,512]{2,1,0:T(8,128)S(1)}, s32[1]{0:T(128)}, ...), condition=%wide.region_1.2_spmd, body=%wide.region_0.1_spmd.sunk | while | flops 33587200 | bytes 13664473 | solution.py:161
  33.4 14.2 %all_to_all.12.parts_ref = f32[8,8,512]{2,1,0:T(8,128)S(1)} all-to-all(f32[8,8,512]{2,1,0:T(8,128)S(1)} %projected.10), channel_id=1, replica_groups=mesh['z'=8,'core'=2,'x'=4,'y'=4] {'z'}, dimensions={0} | all-to-all | bytes 262144 | tf_op jit(solution)/shard_map/while/body/eval_jaxpr/all_to_all | solution.py:149
  80.9 10.3 %all_to_all.12.parts_ref = f32[8,8,512]{2,1,0:T(8,128)S(1)} all-to-all(f32[8,8,512]{2,1,0:T(8,128)S(1)} %projected.10), channel_id=1, replica_groups=mesh['z'=8,'core'=2,'x'=4,'y'=4] {'z'}, dimensions={0} | all-to-all | bytes 262144 | tf_op jit(solution)/shard_map/while/body/eval_jaxpr/all_to_all | solution.py:149
  102.9 10.3 %all_to_all.12.parts_ref = f32[8,8,512]{2,1,0:T(8,128)S(1)} all-to-all(f32[8,8,512]{2,1,0:T(8,128)S(1)} %projected.10), channel_id=1, replica_groups=mesh['z'=8,'core'=2,'x'=4,'y'=4] {'z'}, dimensions={0} | all-to-all | bytes 262144 | tf_op jit(solution)/shard_map/while/body/eval_jaxpr/all_to_all | solution.py:149
  125.0 10.3 %all_to_all.12.parts_ref = f32[8,8,512]{2,1,0:T(8,128)S(1)} all-to-all(f32[8,8,512]{2,1,0:T(8,128)S(1)} %projected.10), channel_id=1, replica_groups=mesh['z'=8,'core'=2,'x'=4,'y'=4] {'z'}, dimensions={0} | all-to-all | bytes 262144 | tf_op jit(solution)/shard_map/while/body/eval_jaxpr/all_to_all | solution.py:149
  147.1 10.3 %all_to_all.12.parts_ref = f32[8,8,512]{2,1,0:T(8,128)S(1)} all-to-all(f32[8,8,512]{2,1,0:T(8,128)S(1)} %projected.10), channel_id=1, replica_groups=mesh['z'=8,'core'=2,'x'=4,'y'=4] {'z'}, dimensions={0} | all-to-all | bytes 262144 | tf_op jit(solution)/shard_map/while/body/eval_jaxpr/all_to_all | solution.py:149
  169.2 10.3 %all_to_all.12.parts_ref = f32[8,8,512]{2,1,0:T(8,128)S(1)} all-to-all(f32[8,8,512]{2,1,0:T(8,128)S(1)} %projected.10), channel_id=1, replica_groups=mesh['z'=8,'core'=2,'x'=4,'y'=4] {'z'}, dimensions={0} | all-to-all | bytes 262144 | tf_op jit(solution)/shard_map/while/body/eval_jaxpr/all_to_all | solution.py:149
  191.2 10.3 %all_to_all.12.parts_ref = f32[8,8,512]{2,1,0:T(8,128)S(1)} all-to-all(f32[8,8,512]{2,1,0:T(8,128)S(1)} %projected.10), channel_id=1, replica_groups=mesh['z'=8,'core'=2,'x'=4,'y'=4] {'z'}, dimensions={0} | all-to-all | bytes 262144 | tf_op jit(solution)/shard_map/while/body/eval_jaxpr/all_to_all | solution.py:149
  213.3 10.3 %all_to_all.12.parts_ref = f32[8,8,512]{2,1,0:T(8,128)S(1)} all-to-all(f32[8,8,512]{2,1,0:T(8,128)S(1)} %projected.10), channel_id=1, replica_groups=mesh['z'=8,'core'=2,'x'=4,'y'=4] {'z'}, dimensions={0} | all-to-all | bytes 262144 | tf_op jit(solution)/shard_map/while/body/eval_jaxpr/all_to_all | solution.py:149
  235.4 10.3 %all_to_all.12.parts_ref = f32[8,8,512]{2,1,0:T(8,128)S(1)} all-to-all(f32[8,8,512]{2,1,0:T(8,128)S(1)} %projected.10), channel_id=1, replica_groups=mesh['z'=8,'core'=2,'x'=4,'y'=4] {'z'}, dimensions={0} | all-to-all | bytes 262144 | tf_op jit(solution)/shard_map/while/body/eval_jaxpr/all_to_all | solution.py:149
  257.4 10.3 %all_to_all.12.parts_ref = f32[8,8,512]{2,1,0:T(8,128)S(1)} all-to-all(f32[8,8,512]{2,1,0:T(8,128)S(1)} %projected.10), channel_id=1, replica_groups=mesh['z'=8,'core'=2,'x'=4,'y'=4] {'z'}, dimensions={0} | all-to-all | bytes 262144 | tf_op jit(solution)/shard_map/while/body/eval_jaxpr/all_to_all | solution.py:149
  279.5 10.3 %all_to_all.12.parts_ref = f32[8,8,512]{2,1,0:T(8,128)S(1)} all-to-all(f32[8,8,512]{2,1,0:T(8,128)S(1)} %projected.10), channel_id=1, replica_groups=mesh['z'=8,'core'=2,'x'=4,'y'=4] {'z'}, dimensions={0} | all-to-all | bytes 262144 | tf_op jit(solution)/shard_map/while/body/eval_jaxpr/all_to_all | solution.py:149
  301.6 10.3 %all_to_all.12.parts_ref = f32[8,8,512]{2,1,0:T(8,128)S(1)} all-to-all(f32[8,8,512]{2,1,0:T(8,128)S(1)} %projected.10), channel_id=1, replica_groups=mesh['z'=8,'core'=2,'x'=4,'y'=4] {'z'}, dimensions={0} | all-to-all | bytes 262144 | tf_op jit(solution)/shard_map/while/body/eval_jaxpr/all_to_all | solution.py:149
  323.7 10.3 %all_to_all.12.parts_ref = f32[8,8,512]{2,1,0:T(8,128)S(1)} all-to-all(f32[8,8,512]{2,1,0:T(8,128)S(1)} %projected.10), channel_id=1, replica_groups=mesh['z'=8,'core'=2,'x'=4,'y'=4] {'z'}, dimensions={0} | all-to-all | bytes 262144 | tf_op jit(solution)/shard_map/while/body/eval_jaxpr/all_to_all | solution.py:149
  345.7 10.3 %all_to_all.12.parts_ref = f32[8,8,512]{2,1,0:T(8,128)S(1)} all-to-all(f32[8,8,512]{2,1,0:T(8,128)S(1)} %projected.10), channel_id=1, replica_groups=mesh['z'=8,'core'=2,'x'=4,'y'=4] {'z'}, dimensions={0} | all-to-all | bytes 262144 | tf_op jit(solution)/shard_map/while/body/eval_jaxpr/all_to_all | solution.py:149
  367.8 10.3 %all_to_all.12.parts_ref = f32[8,8,512]{2,1,0:T(8,128)S(1)} all-to-all(f32[8,8,512]{2,1,0:T(8,128)S(1)} %projected.10), channel_id=1, replica_groups=mesh['z'=8,'core'=2,'x'=4,'y'=4] {'z'}, dimensions={0} | all-to-all | bytes 262144 | tf_op jit(solution)/shard_map/while/body/eval_jaxpr/all_to_all | solution.py:149
  394.8 352.6 %while.35 = (s32[]{:T(128)}, f32[8,2048]{1,0:T(8,128)S(1)}, f32[16,8,512]{2,1,0:T(8,128)S(1)}, s32[1]{0:T(128)}, bf16[2048,512]{1,0:T(8,128)(2,1)S(1)}, /*index=...) while((s32[]{:T(128)}, f32[8,2048]{1,0:T(8,128)S(1)}, ...), condition=%wide.region_3.4_spmd, body=%wide.region_2.3_spmd.sunk | while | flops 33587200 | bytes 13664481 | solution.py:161
  395.6 10.7 %all_to_all.13.parts_ref = f32[8,8,512]{2,1,0:T(8,128)S(1)} all-to-all(f32[8,8,512]{2,1,0:T(8,128)S(1)} %projected.11), channel_id=1, replica_groups=mesh['z'=8,'core'=2,'x'=4,'y'=4] {'z'}, dimensions={0} | all-to-all | bytes 262144 | tf_op jit(solution)/shard_map/while/body/eval_jaxpr/all_to_all | solution.py:149
  417.1 10.3 %all_to_all.13.parts_ref = f32[8,8,512]{2,1,0:T(8,128)S(1)} all-to-all(f32[8,8,512]{2,1,0:T(8,128)S(1)} %projected.11), channel_id=1, replica_groups=mesh['z'=8,'core'=2,'x'=4,'y'=4] {'z'}, dimensions={0} | all-to-all | bytes 262144 | tf_op jit(solution)/shard_map/while/body/eval_jaxpr/all_to_all | solution.py:149
  439.1 10.3 %all_to_all.13.parts_ref = f32[8,8,512]{2,1,0:T(8,128)S(1)} all-to-all(f32[8,8,512]{2,1,0:T(8,128)S(1)} %projected.11), channel_id=1, replica_groups=mesh['z'=8,'core'=2,'x'=4,'y'=4] {'z'}, dimensions={0} | all-to-all | bytes 262144 | tf_op jit(solution)/shard_map/while/body/eval_jaxpr/all_to_all | solution.py:149
  461.2 10.3 %all_to_all.13.parts_ref = f32[8,8,512]{2,1,0:T(8,128)S(1)} all-to-all(f32[8,8,512]{2,1,0:T(8,128)S(1)} %projected.11), channel_id=1, replica_groups=mesh['z'=8,'core'=2,'x'=4,'y'=4] {'z'}, dimensions={0} | all-to-all | bytes 262144 | tf_op jit(solution)/shard_map/while/body/eval_jaxpr/all_to_all | solution.py:149
  483.3 10.3 %all_to_all.13.parts_ref = f32[8,8,512]{2,1,0:T(8,128)S(1)} all-to-all(f32[8,8,512]{2,1,0:T(8,128)S(1)} %projected.11), channel_id=1, replica_groups=mesh['z'=8,'core'=2,'x'=4,'y'=4] {'z'}, dimensions={0} | all-to-all | bytes 262144 | tf_op jit(solution)/shard_map/while/body/eval_jaxpr/all_to_all | solution.py:149
  505.4 10.3 %all_to_all.13.parts_ref = f32[8,8,512]{2,1,0:T(8,128)S(1)} all-to-all(f32[8,8,512]{2,1,0:T(8,128)S(1)} %projected.11), channel_id=1, replica_groups=mesh['z'=8,'core'=2,'x'=4,'y'=4] {'z'}, dimensions={0} | all-to-all | bytes 262144 | tf_op jit(solution)/shard_map/while/body/eval_jaxpr/all_to_all | solution.py:149
  527.4 10.3 %all_to_all.13.parts_ref = f32[8,8,512]{2,1,0:T(8,128)S(1)} all-to-all(f32[8,8,512]{2,1,0:T(8,128)S(1)} %projected.11), channel_id=1, replica_groups=mesh['z'=8,'core'=2,'x'=4,'y'=4] {'z'}, dimensions={0} | all-to-all | bytes 262144 | tf_op jit(solution)/shard_map/while/body/eval_jaxpr/all_to_all | solution.py:149
  549.5 10.3 %all_to_all.13.parts_ref = f32[8,8,512]{2,1,0:T(8,128)S(1)} all-to-all(f32[8,8,512]{2,1,0:T(8,128)S(1)} %projected.11), channel_id=1, replica_groups=mesh['z'=8,'core'=2,'x'=4,'y'=4] {'z'}, dimensions={0} | all-to-all | bytes 262144 | tf_op jit(solution)/shard_map/while/body/eval_jaxpr/all_to_all | solution.py:149
  571.6 10.3 %all_to_all.13.parts_ref = f32[8,8,512]{2,1,0:T(8,128)S(1)} all-to-all(f32[8,8,512]{2,1,0:T(8,128)S(1)} %projected.11), channel_id=1, replica_groups=mesh['z'=8,'core'=2,'x'=4,'y'=4] {'z'}, dimensions={0} | all-to-all | bytes 262144 | tf_op jit(solution)/shard_map/while/body/eval_jaxpr/all_to_all | solution.py:149
  593.6 10.3 %all_to_all.13.parts_ref = f32[8,8,512]{2,1,0:T(8,128)S(1)} all-to-all(f32[8,8,512]{2,1,0:T(8,128)S(1)} %projected.11), channel_id=1, replica_groups=mesh['z'=8,'core'=2,'x'=4,'y'=4] {'z'}, dimensions={0} | all-to-all | bytes 262144 | tf_op jit(solution)/shard_map/while/body/eval_jaxpr/all_to_all | solution.py:149
  615.7 10.3 %all_to_all.13.parts_ref = f32[8,8,512]{2,1,0:T(8,128)S(1)} all-to-all(f32[8,8,512]{2,1,0:T(8,128)S(1)} %projected.11), channel_id=1, replica_groups=mesh['z'=8,'core'=2,'x'=4,'y'=4] {'z'}, dimensions={0} | all-to-all | bytes 262144 | tf_op jit(solution)/shard_map/while/body/eval_jaxpr/all_to_all | solution.py:149
  637.8 10.3 %all_to_all.13.parts_ref = f32[8,8,512]{2,1,0:T(8,128)S(1)} all-to-all(f32[8,8,512]{2,1,0:T(8,128)S(1)} %projected.11), channel_id=1, replica_groups=mesh['z'=8,'core'=2,'x'=4,'y'=4] {'z'}, dimensions={0} | all-to-all | bytes 262144 | tf_op jit(solution)/shard_map/while/body/eval_jaxpr/all_to_all | solution.py:149
  659.9 10.3 %all_to_all.13.parts_ref = f32[8,8,512]{2,1,0:T(8,128)S(1)} all-to-all(f32[8,8,512]{2,1,0:T(8,128)S(1)} %projected.11), channel_id=1, replica_groups=mesh['z'=8,'core'=2,'x'=4,'y'=4] {'z'}, dimensions={0} | all-to-all | bytes 262144 | tf_op jit(solution)/shard_map/while/body/eval_jaxpr/all_to_all | solution.py:149
  704.0 10.3 %all_to_all.13.parts_ref = f32[8,8,512]{2,1,0:T(8,128)S(1)} all-to-all(f32[8,8,512]{2,1,0:T(8,128)S(1)} %projected.11), channel_id=1, replica_groups=mesh['z'=8,'core'=2,'x'=4,'y'=4] {'z'}, dimensions={0} | all-to-all | bytes 262144 | tf_op jit(solution)/shard_map/while/body/eval_jaxpr/all_to_all | solution.py:149
  726.1 10.3 %all_to_all.13.parts_ref = f32[8,8,512]{2,1,0:T(8,128)S(1)} all-to-all(f32[8,8,512]{2,1,0:T(8,128)S(1)} %projected.11), channel_id=1, replica_groups=mesh['z'=8,'core'=2,'x'=4,'y'=4] {'z'}, dimensions={0} | all-to-all | bytes 262144 | tf_op jit(solution)/shard_map/while/body/eval_jaxpr/all_to_all | solution.py:149
  (365 shorter events, 435.4 us)
Async XLA Ops:
  6.0 10.4 %collective-permute-start.5 = (f32[1024,1024]{0,1:T(8,128)}, f32[1024,1024]{0,1:T(8,128)}, u32[]{:S(2)}, u32[]{:S(2)}) collective-permute-start(f32[1024,1024]{0,1:T(8,128)} %convert_element_type.25), channel_id=1, source_target_pairs={{0,16},{16,0},{1,17},{17,1},{2,18},{18,2},{3,19},{19,3},{4,20},{20... | collective-permute-start | bytes 12582920 | tf_op jit(solution)/shard_map/ppermute | solution.py:104
  9.2 7.1 collective-permute-start.4
  51.5 7.0 collective-permute-start.1
  73.6 6.5 collective-permute-start.1
  95.7 6.5 collective-permute-start.1
  117.7 6.5 collective-permute-start.1
  139.8 6.5 collective-permute-start.1
  161.9 6.5 collective-permute-start.1
  184.0 6.5 collective-permute-start.1
  206.0 6.5 collective-permute-start.1
  228.1 6.5 collective-permute-start.1
  250.2 6.5 collective-permute-start.1
  272.2 6.5 collective-permute-start.1
  294.3 6.5 collective-permute-start.1
  316.4 6.5 collective-permute-start.1
  338.5 6.5 collective-permute-start.1
  360.5 6.5 collective-permute-start.1
  382.6 6.5 collective-permute-start.1
  409.8 6.5 collective-permute-start.3
  431.9 6.5 collective-permute-start.3
  453.9 6.5 collective-permute-start.3
  476.0 6.5 collective-permute-start.3
  498.1 6.5 collective-permute-start.3
  520.2 6.5 collective-permute-start.3
  542.2 6.5 collective-permute-start.3
  564.3 6.5 collective-permute-start.3
  586.4 6.5 collective-permute-start.3
  608.4 6.5 collective-permute-start.3
  630.5 6.5 collective-permute-start.3
  652.6 6.5 collective-permute-start.3
  674.7 6.5 collective-permute-start.3
  696.7 6.5 collective-permute-start.3
  (73 other events, 505.4 us)
